TPU v7x, 256 devices: a whole 4x4x8 slice. The times are simulated.
256 devices in a mesh: cls: 2 (over y_hi), dom: 16 (over y_lo, x, core), orient: 8 (over z).
Axes of the slice: x: 4, y: 4 (y_hi: 2, y_lo: 2; y = y_hi * 2 + y_lo), z: 8, core: 2. Of those that a mesh axis runs over, the one named last changes fastest.
Arguments:
- references: bfloat16 [2, 8, 8, 32768], P(None, 'cls', None, ('dom', 'orient')), may hold values from -2 to 2
- images: bfloat16 [2, 2048, 32768], P(None, ('dom', 'orient')), may hold values from -16 to 16
- orient_lists: int32 [2048, 1], P(('dom', 'orient')), may hold values from 0 to 7; in each aligned block of 16 rows (0 to 15, 16 to 31, ...) at most 3 rows name the same one
- shift_ids: int32 [2048, 1], P(('dom', 'orient')), may hold values from 0 to 63
- fixed_weights: float32 [2048, 1], P(('dom', 'orient')), may hold values from 0.2 to 2
Outputs:
- class_prob: float32 [2048, 8], P(('dom', 'orient'), 'cls')
- volume: float32 [2, 8, 8, 32768], P(None, 'cls', 'orient', 'dom')
Inputs may be any that keep to these rules, and one draw needn't show every extreme that they name: `orient_lists`: within the rows of one device (16 particles), no orientation bin is listed by more than 3 particles, a bound that some block reaches.
All inputs are finite; a program needn't handle non-finite values.
Results may differ from a plain program's by a relative error of at most 0.02.
Values may be sent and summed in bfloat16 or wider, within the bound.
A program may use at most 320 MiB of HBM per device.

v0:
```python
import math
import jax
import jax.numpy as jnp
from jax import lax
from jax.sharding import PartitionSpec as P

IMG = 256
TX = 8
TY = 8
TWO_PI = 2.0 * math.pi


def offsets(number):
    return (jnp.arange(number, dtype=jnp.int32) - number // 2).astype(jnp.float32)


def local(references, images, orient_lists, shift_ids, fixed_weights):
    here = images.shape[1]
    classes, orients = (references.shape[1], references.shape[2])
    doms = lax.axis_size("dom")
    band = images.shape[2] // doms
    particles = here * doms
    held = lax.all_to_all(images, "dom", split_axis=2, concat_axis=1, tiled=True)
    piece = lax.all_gather(references, "orient", axis=3, tiled=True)
    ids = lax.all_gather(
        jnp.concatenate([orient_lists, shift_ids], axis=1), "dom", axis=0, tiled=True
    )
    orient_ids, shift_index = (ids[:, 0], ids[:, 1])
    columns = jnp.arange(band, dtype=jnp.int32) + lax.axis_index("dom") * band
    freq_x = (columns % IMG - IMG // 2).astype(jnp.float32)
    freq_y = (columns // IMG).astype(jnp.float32)
    angle_x = TWO_PI / IMG * (offsets(TX)[:, None] * freq_x[None, :])
    angle_y = TWO_PI / IMG * (offsets(TY)[:, None] * freq_y[None, :])
    cx, sx, cy, sy = (jnp.cos(angle_x), jnp.sin(angle_x), jnp.cos(angle_y), jnp.sin(angle_y))
    re, im = (held[0].astype(jnp.float32), held[1].astype(jnp.float32))
    x_re = (re[:, None] * cx - im[:, None] * sx).astype(jnp.bfloat16).reshape(particles * TX, band)
    x_im = (re[:, None] * sx + im[:, None] * cx).astype(jnp.bfloat16).reshape(particles * TX, band)
    r_re = piece[0].reshape(classes * orients, band).astype(jnp.float32)
    r_im = piece[1].reshape(classes * orients, band).astype(jnp.float32)
    s_re = (r_re[None] * cy[:, None] + r_im[None] * sy[:, None]).astype(jnp.bfloat16)
    s_im = (r_im[None] * cy[:, None] - r_re[None] * sy[:, None]).astype(jnp.bfloat16)
    s_re = s_re.reshape(TY * classes * orients, band)
    s_im = s_im.reshape(TY * classes * orients, band)
    part = jnp.einsum("aj,bj->ab", x_re, s_re, preferred_element_type=jnp.float32)
    part = part + jnp.einsum("aj,bj->ab", x_im, s_im, preferred_element_type=jnp.float32)
    part = lax.all_to_all(
        part.reshape(doms, here * TX, -1), "dom", split_axis=0, concat_axis=0, tiled=True
    )
    logits = jnp.sum(part, axis=0).reshape(here, TX, TY, classes, orients)
    top = jnp.max(logits, axis=(1, 2, 3, 4))
    top = lax.pmax(top, "cls")
    exponent = jnp.exp(logits - top[:, None, None, None, None])
    sums = jnp.sum(exponent, axis=(1, 2, 4))
    totals = lax.psum(jnp.sum(sums, axis=1), "cls")
    class_prob = sums / totals[:, None]
    weight = (fixed_weights * class_prob).astype(jnp.bfloat16)
    weight = lax.all_gather(weight, "dom", axis=0, tiled=True)
    entry_x = (shift_index % TX - TX // 2).astype(jnp.float32)
    entry_y = (shift_index // TX - TY // 2).astype(jnp.float32)
    angle = TWO_PI / IMG * (entry_x[:, None] * freq_x[None] + entry_y[:, None] * freq_y[None])
    cosine, sine = (jnp.cos(angle), jnp.sin(angle))
    row_re = (re * cosine - im * sine).astype(jnp.bfloat16)
    row_im = (re * sine + im * cosine).astype(jnp.bfloat16)
    onehot = (orient_ids[:, None] == jnp.arange(orients, dtype=jnp.int32)[None]).astype(
        jnp.bfloat16
    )
    mixing = (onehot[:, :, None] * weight[:, None, :]).reshape(particles, orients * classes)
    grown = [
        jnp.einsum("pm,pj->mj", mixing, row, preferred_element_type=jnp.float32).reshape(
            orients, 1, classes, band
        )
        for row in (row_re, row_im)
    ]
    grown = jnp.concatenate(grown, axis=1)
    grown = lax.all_to_all(grown, "orient", split_axis=0, concat_axis=0, tiled=True)
    volume = jnp.sum(grown, axis=0)[:, :, None, :]
    return (class_prob, volume)


def solution(mesh):
    in_specs = (
        P(None, "cls", None, ("dom", "orient")),
        P(None, ("dom", "orient"), None),
        P(("dom", "orient"), None),
        P(("dom", "orient"), None),
        P(("dom", "orient"), None),
    )
    out_specs = (P(("dom", "orient"), "cls"), P(None, "cls", "orient", "dom"))
    return jax.shard_map(local, mesh=mesh, in_specs=in_specs, out_specs=out_specs, check_vma=False)
```

profile of v0, /device:TPU:1, one launch (start us, length us, event | category | flops | bytes accessed | tf_op | source)
XLA Modules:
  0.0 253.7 jit_solution(4576734842398924274)
XLA Ops:
  0.6 30.9 %copy.31 = bf16[2,16,32768]{1,0,2:T(2,128)(2,1)} copy(bf16[2,16,32768]{2,1,0:T(8,128)(2,1)} %param.6) | data formatting | bytes 4194304 | tf_op args[1]
  31.5 20.8 %reshape.408 = bf16[16,2,32768]{2,1,0:T(2,128)(2,1)} reshape(bf16[32768,2,16]{2,1,0:T(2,128)(2,1)} %bitcast.57) | data formatting | bytes 4194304
  52.3 7.0 %all-to-all-start = ((bf16[16,2,32768]{2,1,0:T(2,128)(2,1)}), bf16[16,2,32768]{2,1,0:T(2,128)(2,1)S(1)}, u32[]{:S(2)}, u32[]{:S(2)}) async-start(bf16[16,2,32768]{2,1,0:T(2,128)(2,1)} %reshape.408), calls=%async_computation | async-start | bytes 4194304 | tf_op jit(solution)/shard_map/all_to_all | solution.py:23
  59.3 24.1 %all_gather.9 = bf16[2,4,8,2048]{3,2,1,0:T(8,128)(2,1)S(1)} all-gather(bf16[2,4,8,256]{3,2,1,0:T(8,128)(2,1)S(1)} %copy-done.1), channel_id=1, replica_groups=mesh['cls'=2,'dom'=16,'orient'=8] {'orient'}, dimensions={3}, use_global_device_ids=true | all-gather | bytes 294912 | tf_op jit(solution)/shard_map/all_gather | solution.py:24
  83.5 0.5 fusion.24
  84.0 1.5 subtract_convert_fusion.2
  85.6 1.3 all-to-all-done
  86.9 14.4 %reshape.409 = bf16[32768,2,16]{2,1,0:T(2,128)(2,1)} reshape(bf16[16,2,32768]{2,1,0:T(2,128)(2,1)S(1)} %all-to-all-done) | data formatting | bytes 4194304
  101.3 23.3 %copy.45 = bf16[2,16,16,2048]{3,2,1,0:T(8,128)(2,1)S(1)} copy(bf16[2,16,16,2048]{1,0,3,2:T(2,128)(2,1)} %bitcast.56) | data formatting | bytes 4194304 | tf_op jit(solution)/shard_map/all_to_all | solution.py:23
  124.6 0.5 slice_convert_fusion.1
  125.2 1.2 copy.33
  126.4 1.2 copy.34
  127.6 2.8 %fusion.1 = f32[2048,256]{1,0:T(8,128)S(1)} fusion(bf16[256,2048]{1,0:T(8,128)(2,1)S(1)} %bitcast.68, f32[8,2048]{1,0:T(8,128)S(1)} %get-tuple-element.15, f32[256,2048]{1,0:T(8,128)S(1)} %bitcast.65, f32[8,2048]{1,0:T(8,128)S(1)} %get-tuple-element.14, f32[256,2048]{1,0:T(8,128)S(1)} %bitcast.63), kind=kOutput, calls=%fused_computation.3 | convolution fusion | flops 2164260864 | bytes 7471104 | tf_op jit(solution)/shard_map/aj,bj->ab/dot_general | solution.py:44
  130.4 3.9 %fusion.14 = f32[2048,256]{1,0:T(8,128)} fusion(f32[2048,256]{1,0:T(8,128)S(1)} %fusion.1, bf16[256,2048]{1,0:T(8,128)(2,1)S(1)} %bitcast.67, f32[8,2048]{1,0:T(8,128)S(1)} %get-tuple-element.15, f32[256,2048]{1,0:T(8,128)S(1)} %bitcast.66, f32[8,2048]{1,0:T(8,128)S(1)} %get-tuple-element.14, f32[256,2048]{1,0:T(8,128)S(1)} %bitcast.64), kind=kOutput, calls=%fused_computation.14 | convolution fusion | flops 2164785152 | bytes 9568256 | tf_op jit(solution)/shard_map/aj,bj->ab/dot_general | solution.py:45
  134.3 8.8 %all-to-all-start.1 = ((f32[16,128,256]{2,1,0:T(8,128)}), f32[16,128,256]{2,1,0:T(8,128)}, u32[]{:S(2)}, u32[]{:S(2)}) async-start(f32[16,128,256]{2,1,0:T(8,128)} %bitcast.62), calls=%async_computation.1 | async-start | bytes 4194304 | tf_op jit(solution)/shard_map/all_to_all | solution.py:46
  143.1 40.1 %all-gather = s32[16,16,2]{1,2,0:T(2,128)S(1)} all-gather(s32[1,16,2]{1,2,0:T(2,128)S(1)} %add_bitcast_fusion), channel_id=1, replica_groups=mesh['cls'=2,'dom'=16,'orient'=8] {'dom'}, dimensions={0}, use_global_device_ids=true | all-gather | bytes 2176 | tf_op jit(solution)/shard_map/all_gather | solution.py:25
  183.3 0.1 reshape.391
  183.4 0.1 mul.358
  183.5 0.1 copy.38
  183.5 0.1 mul.362
  183.6 0.1 copy.39
  183.7 8.7 %subtract_convert_fusion.1 = (bf16[1,16,16,2048]{3,1,2,0:T(8,128)(2,1)S(1)}, bf16[1,16,16,2048]{3,1,2,0:T(8,128)(2,1)S(1)}) fusion(f32[2048]{0:T(1024)S(1)} %get-tuple-element.23, f32[16,16]{0,1:T(8,128)S(1)} %copy.39, f32[2048]{0:T(1024)S(1)} %get-tuple-element.22, f32[16,16]{0,1:T(8,128)S(1)} %copy.38, bf16[2,16,16,2048]{3,1,2,0:T(8,128)(2,1)S(1)} %bitcast.59), kind=kLoop, calls=%fused_computation.18 | loop fusion | flops 7340032 | bytes 4212736 | tf_op jit(solution)/shard_map/convert_element_type | solution.py:62
  192.4 0.6 copy.40
  193.0 1.6 copy.42
  194.6 0.0 all-to-all-done.1
  194.6 1.7 reduce_sum.43
  196.3 0.1 copy.35
  196.4 0.1 reduce_max.10
  196.5 0.1 reduce_max.14
  196.6 0.1 reduce_max.18
  196.7 5.3 %pmax.7 = f32[16]{0:T(128)S(1)} all-reduce(f32[16]{0:T(128)S(1)} %reduce_max.18), channel_id=1, replica_groups=mesh['cls'=2,'dom'=16,'orient'=8] {'cls'}, use_global_device_ids=true, to_apply=%region_3.4 | all-reduce | flops 16 | bytes 128 | tf_op jit(solution)/shard_map/pmax | solution.py:51
  202.0 0.1 sub.78
  202.1 0.1 sub.79
  202.2 0.2 exponential_reduce_fusion.1
  202.4 0.1 reduce_sum.46
  202.5 0.1 reduce_sum.47
  202.6 5.3 %psum.7 = f32[16]{0:T(128)S(1)} all-reduce(f32[16]{0:T(128)S(1)} %reduce_sum.47), channel_id=1, replica_groups=mesh['cls'=2,'dom'=16,'orient'=8] {'cls'}, use_global_device_ids=true, to_apply=%region_7.8 | all-reduce | flops 16 | bytes 128 | tf_op jit(solution)/shard_map/psum | solution.py:54
  207.9 1.1 reshape.384
  209.0 0.5 exponential_reduce_fusion
  209.5 0.6 fusion.36
  210.1 18.2 %all-gather.1 = bf16[16,16,4]{1,2,0:T(4,128)(2,1)S(1)} all-gather(bf16[1,16,4]{1,2,0:T(4,128)(2,1)S(1)} %get-tuple-element.4), channel_id=1, replica_groups=mesh['cls'=2,'dom'=16,'orient'=8] {'dom'}, dimensions={0}, use_global_device_ids=true | all-gather | bytes 2176 | tf_op jit(solution)/shard_map/all_gather | solution.py:57
  228.4 0.1 reshape.393
  228.6 0.3 convolution_bitcast_fusion.1
  228.8 1.5 convolution_bitcast_fusion
  230.4 0.3 copy.44
  230.7 22.2 %all_to_all.25 = f32[8,2,4,2048]{3,2,1,0:T(4,128)S(1)} all-to-all(f32[8,2,4,2048]{3,2,1,0:T(4,128)S(1)} %copy.44), channel_id=1, replica_groups=mesh['cls'=2,'dom'=16,'orient'=8] {'orient'}, dimensions={0} | all-to-all | bytes 1048576 | tf_op jit(solution)/shard_map/all_to_all | solution.py:75
  253.0 0.1 reduce_sum.48
  253.1 0.7 broadcast_in_dim.2
  (23 shorter events, 0.2 us)
Async XLA Ops:
  52.3 7.0 %copy-start.1 = (bf16[2,4,8,256]{3,2,1,0:T(8,128)(2,1)S(1)}, bf16[2,4,8,256]{3,2,1,0:T(8,128)(2,1)}, u32[]{:S(2)}) copy-start(bf16[2,4,8,256]{3,2,1,0:T(8,128)(2,1)} %param.5) | copy-start | bytes 98308
  52.3 34.6 %all-to-all-start = ((bf16[16,2,32768]{2,1,0:T(2,128)(2,1)}), bf16[16,2,32768]{2,1,0:T(2,128)(2,1)S(1)}, u32[]{:S(2)}, u32[]{:S(2)}) async-start(bf16[16,2,32768]{2,1,0:T(2,128)(2,1)} %reshape.408), calls=%async_computation | async-start | bytes 4194304 | tf_op jit(solution)/shard_map/all_to_all | solution.py:23
  126.4 1.2 copy-start
  134.3 8.8 %copy-start.3 = (s32[16,1]{0,1:T(1,128)S(1)}, s32[16,1]{0,1:T(1,128)}, u32[]{:S(2)}) copy-start(s32[16,1]{0,1:T(1,128)} %param.8) | copy-start | bytes 196
  134.3 8.8 %copy-start.4 = (s32[16,1]{0,1:T(1,128)S(1)}, s32[16,1]{0,1:T(1,128)}, u32[]{:S(2)}) copy-start(s32[16,1]{0,1:T(1,128)} %param.7) | copy-start | bytes 196
  134.3 60.3 %all-to-all-start.1 = ((f32[16,128,256]{2,1,0:T(8,128)}), f32[16,128,256]{2,1,0:T(8,128)}, u32[]{:S(2)}, u32[]{:S(2)}) async-start(f32[16,128,256]{2,1,0:T(8,128)} %bitcast.62), calls=%async_computation.1 | async-start | bytes 4194304 | tf_op jit(solution)/shard_map/all_to_all | solution.py:46
  207.9 1.6 copy-start.2
where the time goes:
time: 258 us; the launch traced here: 254 us
  blocking collectives  115 us (45%)
  local copies, waits for them, and re-layouts  97 us (38%)
  starting transfers between devices  15.7 us (6%)
  other arithmetic  15 us (6%)
  matrix products  8.47 us (3%)
    unnamed x15, local copies, waits for them, and re-layouts  66.2 us
    all_gather x1, blocking collectives, local(): lax.all_gather(jnp.concatenate([orient_lists, shift_ids], axis=1), 'dom',...  40.1 us
    all_gather x1, blocking collectives, local(): piece = lax.all_gather(references, 'orient', axis=3, tiled=True)  24.1 us
    all_to_all x1, local copies, waits for them, and re-layouts, local(): lax.all_to_all(images, 'dom', split_axis=2, concat_axis=1, tiled=True)  23.3 us
    all_to_all x1, blocking collectives, local(): lax.all_to_all(grown, 'orient', split_axis=0, concat_axis=0, tiled=True)  22.2 us
    all_gather x1, blocking collectives, local(): weight = lax.all_gather(weight, 'dom', axis=0, tiled=True)  18.2 us
    all_to_all x1, starting transfers between devices, local(): lax.all_to_all(part.reshape(doms, here * TX, -1), 'dom', split_axis=0, co...  8.77 us
    convert_element_type x1, other arithmetic, local(): row_re = (re * cosine - im * sine).astype(jnp.bfloat16)  8.74 us
  transfers between devices with their start and end apart: 2, of which 1 were waited for; matrix products, arithmetic and copies ran while one was open for 5% of the time, Pallas kernels for 0%

commit v1 on v0

--- a/solution.py
+++ b/solution.py
@@ -21,7 +21,8 @@
     band = images.shape[2] // doms
     particles = here * doms
     held = lax.all_to_all(images, "dom", split_axis=2, concat_axis=1, tiled=True)
-    piece = lax.all_gather(references, "orient", axis=3, tiled=True)
+    repeated = jnp.stack([references] * lax.axis_size("orient"))
+    piece = jnp.concatenate(lax.all_to_all(repeated, "orient", 0, 0), axis=3)
     ids = lax.all_gather(
         jnp.concatenate([orient_lists, shift_ids], axis=1), "dom", axis=0, tiled=True
     )

time: 258 us -> 267 us (1.035)
  waiting for transfers between devices: 1.35 us -> 25 us
  blocking collectives: 115 us -> 93.6 us
  starting transfers between devices: 15.7 us -> 20.4 us
    all_gather x1 -> x0, blocking collectives: 24.1 us -> none  [local(): piece = lax.all_gather(references, 'orient', axis=3, tiled=True)]
    all_to_all x1, waiting for transfers between devices: 1.35 us -> 25 us  [local(): lax.all_to_all(images, 'dom', split_axis=2, concat_axis=1, tiled=True)]
    all_to_all x0 -> x1, starting transfers between devices: none -> 9.01 us  [local(): piece = jnp.concatenate(lax.all_to_all(repeated, 'orient', 0, 0), axis=3)]
    all_to_all x1, starting transfers between devices: 8.77 us -> 5.08 us  [local(): lax.all_to_all(part.reshape(doms, here * TX, -1), 'dom', split_axis=0, co...]
    unnamed x15 -> x16, local copies, waits for them, and re-layouts: 66.2 us -> 66.7 us
  transfers between devices with their start and end apart: 2 -> 3, of which waited for: 1 -> 1; matrix products, arithmetic and copies ran while one was open for 5% -> 25% of each run, Pallas kernels for 0% -> 0%
where the time goes in v1:
time: 267 us; the launch traced here: 262 us
  local copies, waits for them, and re-layouts  99 us (37%)
  blocking collectives  93.6 us (35%)
  waiting for transfers between devices  25 us (9%)
  starting transfers between devices  20.4 us (8%)
  other arithmetic  15 us (6%)
  matrix products  8.47 us (3%)
    unnamed x16, local copies, waits for them, and re-layouts  66.7 us
    all_gather x1, blocking collectives, local(): lax.all_gather(jnp.concatenate([orient_lists, shift_ids], axis=1), 'dom',...  40.1 us
    all_to_all x1, waiting for transfers between devices, local(): lax.all_to_all(images, 'dom', split_axis=2, concat_axis=1, tiled=True)  25 us
    all_to_all x1, blocking collectives, local(): lax.all_to_all(grown, 'orient', split_axis=0, concat_axis=0, tiled=True)  24.6 us
    all_to_all x1, local copies, waits for them, and re-layouts, local(): lax.all_to_all(images, 'dom', split_axis=2, concat_axis=1, tiled=True)  23.3 us
    all_gather x1, blocking collectives, local(): weight = lax.all_gather(weight, 'dom', axis=0, tiled=True)  18.2 us
    all_to_all x1, starting transfers between devices, local(): piece = jnp.concatenate(lax.all_to_all(repeated, 'orient', 0, 0), axis=3)  9.01 us
    convert_element_type x1, other arithmetic, local(): row_re = (re * cosine - im * sine).astype(jnp.bfloat16)  8.74 us
  transfers between devices with their start and end apart: 3, of which 1 were waited for; matrix products, arithmetic and copies ran while one was open for 25% of the time, Pallas kernels for 0%

profile of v1, /device:TPU:1, one launch (start us, length us, event | category | flops | bytes accessed | tf_op | source)
XLA Modules:
  0.0 262.2 jit_solution(13225554381849066761)
XLA Ops:
  0.6 1.5 stack.2
  2.1 9.0 %all-to-all-start.1 = ((bf16[8,2,4,8,256]{4,3,2,1,0:T(8,128)(2,1)}), bf16[8,2,4,8,256]{4,3,2,1,0:T(8,128)(2,1)S(1)}, u32[]{:S(2)}, u32[]{:S(2)}) async-start(bf16[8,2,4,8,256]{4,3,2,1,0:T(8,128)(2,1)} %stack.2), calls=%async_computation.1 | async-start | bytes 524288 | tf_op jit(solution)/shard_map/all_to_all | solution.py:25
  11.1 30.9 %copy.31 = bf16[2,16,32768]{1,0,2:T(2,128)(2,1)} copy(bf16[2,16,32768]{2,1,0:T(8,128)(2,1)} %param.6) | data formatting | bytes 4194304 | tf_op args[1]
  42.0 20.8 %reshape.419 = bf16[16,2,32768]{2,1,0:T(2,128)(2,1)} reshape(bf16[32768,2,16]{2,1,0:T(2,128)(2,1)} %bitcast.56) | data formatting | bytes 4194304
  62.8 6.3 %all-to-all-start = ((bf16[16,2,32768]{2,1,0:T(2,128)(2,1)}), bf16[16,2,32768]{2,1,0:T(2,128)(2,1)S(1)}, u32[]{:S(2)}, u32[]{:S(2)}) async-start(bf16[16,2,32768]{2,1,0:T(2,128)(2,1)} %reshape.419), calls=%async_computation | async-start | bytes 4194304 | tf_op jit(solution)/shard_map/all_to_all | solution.py:23
  69.1 0.5 fusion.22
  69.7 0.3 copy_bitcast_fusion
  70.0 0.1 copy.48
  70.1 0.1 copy.49
  70.2 1.5 subtract_convert_fusion.2
  71.8 25.0 %all-to-all-done = bf16[16,2,32768]{2,1,0:T(2,128)(2,1)S(1)} async-done(((bf16[16,2,32768]{2,1,0:T(2,128)(2,1)}), bf16[16,2,32768]{2,1,0:T(2,128)(2,1)S(1)}, u32[]{:S(2)}, u32[]{:S(2)}) %all-to-all-start) | async-done | bytes 2097184 | tf_op jit(solution)/shard_map/all_to_all | solution.py:23
  96.8 14.4 %reshape.420 = bf16[32768,2,16]{2,1,0:T(2,128)(2,1)} reshape(bf16[16,2,32768]{2,1,0:T(2,128)(2,1)S(1)} %all-to-all-done) | data formatting | bytes 4194304
  111.2 23.3 %copy.47 = bf16[2,16,16,2048]{3,2,1,0:T(8,128)(2,1)S(1)} copy(bf16[2,16,16,2048]{1,0,3,2:T(2,128)(2,1)} %bitcast.55) | data formatting | bytes 4194304 | tf_op jit(solution)/shard_map/all_to_all | solution.py:23
  134.5 0.5 slice_convert_fusion.1
  135.0 1.2 copy.33
  136.2 1.2 copy.34
  137.5 2.8 %fusion.1 = f32[2048,256]{1,0:T(8,128)S(1)} fusion(bf16[256,2048]{1,0:T(8,128)(2,1)S(1)} %bitcast.68, f32[8,2048]{1,0:T(8,128)S(1)} %get-tuple-element.15, f32[256,2048]{1,0:T(8,128)S(1)} %bitcast.64, f32[8,2048]{1,0:T(8,128)S(1)} %get-tuple-element.14, f32[256,2048]{1,0:T(8,128)S(1)} %bitcast.62), kind=kOutput, calls=%fused_computation.3 | convolution fusion | flops 2164260864 | bytes 7471104 | tf_op jit(solution)/shard_map/aj,bj->ab/dot_general | solution.py:45
  140.2 3.9 %fusion.14 = f32[2048,256]{1,0:T(8,128)} fusion(f32[2048,256]{1,0:T(8,128)S(1)} %fusion.1, bf16[256,2048]{1,0:T(8,128)(2,1)S(1)} %bitcast.67, f32[8,2048]{1,0:T(8,128)S(1)} %get-tuple-element.15, f32[256,2048]{1,0:T(8,128)S(1)} %bitcast.65, f32[8,2048]{1,0:T(8,128)S(1)} %get-tuple-element.14, f32[256,2048]{1,0:T(8,128)S(1)} %bitcast.63), kind=kOutput, calls=%fused_computation.14 | convolution fusion | flops 2164785152 | bytes 9568256 | tf_op jit(solution)/shard_map/aj,bj->ab/dot_general | solution.py:46
  144.2 5.1 %all-to-all-start.2 = ((f32[16,128,256]{2,1,0:T(8,128)}), f32[16,128,256]{2,1,0:T(8,128)}, u32[]{:S(2)}, u32[]{:S(2)}) async-start(f32[16,128,256]{2,1,0:T(8,128)} %bitcast.61), calls=%async_computation.2 | async-start | bytes 4194304 | tf_op jit(solution)/shard_map/all_to_all | solution.py:47
  149.3 40.1 %all-gather = s32[16,16,2]{1,2,0:T(2,128)S(1)} all-gather(s32[1,16,2]{1,2,0:T(2,128)S(1)} %add_bitcast_fusion), channel_id=1, replica_groups=mesh['cls'=2,'dom'=16,'orient'=8] {'dom'}, dimensions={0}, use_global_device_ids=true | all-gather | bytes 2176 | tf_op jit(solution)/shard_map/all_gather | solution.py:26
  189.4 0.1 reshape.402
  189.5 0.1 mul.358
  189.7 0.1 mul.362
  189.9 8.7 %subtract_convert_fusion.1 = (bf16[1,16,16,2048]{3,1,2,0:T(8,128)(2,1)S(1)}, bf16[1,16,16,2048]{3,1,2,0:T(8,128)(2,1)S(1)}) fusion(f32[2048]{0:T(1024)S(1)} %get-tuple-element.23, f32[16,16]{0,1:T(8,128)S(1)} %copy.41, f32[2048]{0:T(1024)S(1)} %get-tuple-element.22, f32[16,16]{0,1:T(8,128)S(1)} %copy.40, bf16[2,16,16,2048]{3,1,2,0:T(8,128)(2,1)S(1)} %bitcast.58), kind=kLoop, calls=%fused_computation.18 | loop fusion | flops 7340032 | bytes 4212736 | tf_op jit(solution)/shard_map/convert_element_type | solution.py:63
  198.6 0.6 copy.42
  199.2 1.6 copy.44
  200.7 1.7 reduce_sum.43
  202.5 0.1 copy.37
  202.6 0.1 reduce_max.10
  202.7 0.1 reduce_max.14
  202.8 0.1 reduce_max.18
  202.9 5.3 %pmax.7 = f32[16]{0:T(128)S(1)} all-reduce(f32[16]{0:T(128)S(1)} %reduce_max.18), channel_id=1, replica_groups=mesh['cls'=2,'dom'=16,'orient'=8] {'cls'}, use_global_device_ids=true, to_apply=%region_3.4 | all-reduce | flops 16 | bytes 128 | tf_op jit(solution)/shard_map/pmax | solution.py:52
  208.3 0.1 sub.79
  208.4 0.2 exponential_reduce_fusion.1
  208.5 0.1 reduce_sum.46
  208.6 0.1 reduce_sum.47
  208.8 5.3 %psum.7 = f32[16]{0:T(128)S(1)} all-reduce(f32[16]{0:T(128)S(1)} %reduce_sum.47), channel_id=1, replica_groups=mesh['cls'=2,'dom'=16,'orient'=8] {'cls'}, use_global_device_ids=true, to_apply=%region_7.8 | all-reduce | flops 16 | bytes 128 | tf_op jit(solution)/shard_map/psum | solution.py:55
  214.1 1.1 reshape.395
  215.2 0.5 exponential_reduce_fusion
  215.7 0.6 fusion.34
  216.3 18.2 %all-gather.1 = bf16[16,16,4]{1,2,0:T(4,128)(2,1)S(1)} all-gather(bf16[1,16,4]{1,2,0:T(4,128)(2,1)S(1)} %get-tuple-element.4), channel_id=1, replica_groups=mesh['cls'=2,'dom'=16,'orient'=8] {'dom'}, dimensions={0}, use_global_device_ids=true | all-gather | bytes 2176 | tf_op jit(solution)/shard_map/all_gather | solution.py:58
  234.6 0.1 reshape.404
  234.7 0.3 convolution_bitcast_fusion.1
  235.0 1.5 convolution_bitcast_fusion
  236.5 0.3 copy.46
  236.9 24.6 %all_to_all.30 = f32[8,2,4,2048]{3,2,1,0:T(4,128)S(1)} all-to-all(f32[8,2,4,2048]{3,2,1,0:T(4,128)S(1)} %copy.46), channel_id=1, replica_groups=mesh['cls'=2,'dom'=16,'orient'=8] {'orient'}, dimensions={0} | all-to-all | bytes 1048576 | tf_op jit(solution)/shard_map/all_to_all | solution.py:76
  261.5 0.1 reduce_sum.48
  261.6 0.7 broadcast_in_dim.2
  (26 shorter events, 0.4 us)
Async XLA Ops:
  2.1 60.7 %all-to-all-start.1 = ((bf16[8,2,4,8,256]{4,3,2,1,0:T(8,128)(2,1)}), bf16[8,2,4,8,256]{4,3,2,1,0:T(8,128)(2,1)S(1)}, u32[]{:S(2)}, u32[]{:S(2)}) async-start(bf16[8,2,4,8,256]{4,3,2,1,0:T(8,128)(2,1)} %stack.2), calls=%async_computation.1 | async-start | bytes 524288 | tf_op jit(solution)/shard_map/all_to_all | solution.py:25
  62.8 34.0 %all-to-all-start = ((bf16[16,2,32768]{2,1,0:T(2,128)(2,1)}), bf16[16,2,32768]{2,1,0:T(2,128)(2,1)S(1)}, u32[]{:S(2)}, u32[]{:S(2)}) async-start(bf16[16,2,32768]{2,1,0:T(2,128)(2,1)} %reshape.419), calls=%async_computation | async-start | bytes 4194304 | tf_op jit(solution)/shard_map/all_to_all | solution.py:23
  136.2 1.2 copy-start
  144.2 5.1 %copy-start.2 = (s32[16,1]{0,1:T(1,128)S(1)}, s32[16,1]{0,1:T(1,128)}, u32[]{:S(2)}) copy-start(s32[16,1]{0,1:T(1,128)} %param.8) | copy-start | bytes 196
  144.2 5.1 %copy-start.3 = (s32[16,1]{0,1:T(1,128)S(1)}, s32[16,1]{0,1:T(1,128)}, u32[]{:S(2)}) copy-start(s32[16,1]{0,1:T(1,128)} %param.7) | copy-start | bytes 196
  144.2 56.6 %all-to-all-start.2 = ((f32[16,128,256]{2,1,0:T(8,128)}), f32[16,128,256]{2,1,0:T(8,128)}, u32[]{:S(2)}, u32[]{:S(2)}) async-start(f32[16,128,256]{2,1,0:T(8,128)} %bitcast.61), calls=%async_computation.2 | async-start | bytes 4194304 | tf_op jit(solution)/shard_map/all_to_all | solution.py:47
  214.1 1.6 copy-start.1
